TPU v7x, 512 devices: a whole 4x4x16 slice. The times are simulated.
512 devices in a mesh: dp: 8 (over y, core), seq: 64 (over x, z).
Axes of the slice: x: 4, y: 4, z: 16, core: 2. Of those that a mesh axis runs over, the one named last changes fastest.
Arguments:
- queries: bfloat16 [8, 4096, 8192], P('dp', 'seq'), may hold values from -8 to 8
- keys: bfloat16 [8, 4096, 1024], P('dp', 'seq'), may hold values from -8 to 8
- values: bfloat16 [8, 4096, 1024], P('dp', 'seq'), may hold values from -6 to 6
- doc_lengths: int32 [8, 129], replicated, may hold values from 0 to 2048, as said below
Outputs:
- attended: bfloat16 [8, 4096, 8192], P('dp', 'seq')
Inputs may be any that keep to these rules, and one draw needn't show every extreme that they name: `doc_lengths`: each row sums to 4096; zeros stand only after the last document; the first document of every row has 32 tokens and the second exactly 2048.
All inputs are finite; a program needn't handle non-finite values.
Results may differ from a plain program's by a relative error of at most 0.0045.
Values may be sent and summed in bfloat16 or wider, within the bound.
A program may use at most 64 MiB of HBM per device.

v0:
```python
import math

import jax
import jax.numpy as jnp
from jax import lax
from jax.sharding import PartitionSpec as P

QH = 64
KVH = 8
HD = 128
GROUP = 8


def doc_starts(lengths_row, positions):
    doc_ends = jnp.cumsum(lengths_row)
    return jnp.max(jnp.where(doc_ends[None, :] <= positions[:, None], doc_ends, 0), axis=1)


def attend_blocks(
    head_queries, head_keys, head_values, lengths_row, block_list, block_rows, key_rows
):
    heads_here = head_queries.shape[1]
    score_scale = 1.0 / math.sqrt(HD)

    def one_block(block_index):
        first_row = block_index * block_rows
        query_block = lax.dynamic_slice_in_dim(head_queries, first_row, block_rows, 0)
        positions = first_row + jnp.arange(block_rows, dtype=jnp.int32)
        starts = doc_starts(lengths_row, positions)
        first_block = jnp.min(starts) // key_rows
        last_block = (first_row + block_rows - 1) // key_rows

        def tile(index):
            key_start = (index * key_rows).astype(jnp.int32)
            key_tile = lax.dynamic_slice_in_dim(head_keys, key_start, key_rows, 0)
            key_positions = key_start + jnp.arange(key_rows, dtype=jnp.int32)
            allowed = (key_positions[None, :] >= starts[:, None]) & (
                key_positions[None, :] <= positions[:, None]
            )
            scores = (
                jnp.einsum(
                    "qhd,thd->hqt", query_block, key_tile, preferred_element_type=jnp.float32
                )
                * score_scale
            )
            return (scores, allowed, key_start)

        def peak_step(index, peak):
            scores, allowed, key_start = tile(index)
            return jnp.maximum(peak, jnp.max(jnp.where(allowed[None], scores, -jnp.inf), axis=-1))

        peak = lax.fori_loop(
            first_block,
            last_block + 1,
            peak_step,
            jnp.full((heads_here, block_rows), -jnp.inf, jnp.float32),
        )

        def sum_step(index, carry):
            total, summed = carry
            scores, allowed, key_start = tile(index)
            weights = jnp.where(allowed[None], jnp.exp(scores - peak[..., None]), 0.0).astype(
                jnp.bfloat16
            )
            value_tile = lax.dynamic_slice_in_dim(head_values, key_start, key_rows, 0)
            total = total + jnp.sum(weights.astype(jnp.float32), axis=-1)
            summed = summed + jnp.einsum(
                "hqt,thd->qhd", weights, value_tile, preferred_element_type=jnp.float32
            )
            return (total, summed)

        total, summed = lax.fori_loop(
            first_block,
            last_block + 1,
            sum_step,
            (
                jnp.zeros((heads_here, block_rows), jnp.float32),
                jnp.zeros((block_rows, heads_here, HD), jnp.float32),
            ),
        )
        return (summed / jnp.transpose(total)[:, :, None]).astype(jnp.bfloat16)

    return lax.map(one_block, block_list)


def per_device(queries, keys, values, doc_lengths):
    tokens_here = queries.shape[1]
    seq_count = lax.axis_size("seq")
    lengths_row = lax.dynamic_index_in_dim(doc_lengths, lax.axis_index("dp"), 0, keepdims=False)
    heads_here = QH // seq_count
    query_split = queries[0].reshape(tokens_here, seq_count, heads_here, HD)
    key_split = jnp.repeat(keys[0].reshape(tokens_here, KVH, HD), GROUP, axis=1).reshape(
        tokens_here, seq_count, heads_here, HD
    )
    value_split = jnp.repeat(values[0].reshape(tokens_here, KVH, HD), GROUP, axis=1).reshape(
        tokens_here, seq_count, heads_here, HD
    )
    head_queries, head_keys, head_values = (
        lax.all_to_all(query_split, "seq", split_axis=1, concat_axis=0, tiled=True),
        lax.all_to_all(key_split, "seq", split_axis=1, concat_axis=0, tiled=True),
        lax.all_to_all(value_split, "seq", split_axis=1, concat_axis=0, tiled=True),
    )
    length = tokens_here * seq_count
    head_queries = head_queries.reshape(length, heads_here, HD)
    head_keys = head_keys.reshape(length, heads_here, HD)
    head_values = head_values.reshape(length, heads_here, HD)
    block_rows = min(512, length // 2)
    key_rows = block_rows // 2
    block_count = length // block_rows
    result = attend_blocks(
        head_queries,
        head_keys,
        head_values,
        lengths_row,
        jnp.arange(block_count, dtype=jnp.int32),
        block_rows,
        key_rows,
    ).reshape(length, 1, heads_here, HD)
    returned_rows = lax.all_to_all(result, "seq", split_axis=0, concat_axis=1, tiled=True)
    return returned_rows.reshape(1, tokens_here, QH * HD)


def solution(mesh):
    placed = (P("dp", "seq", None), P("dp", "seq", None), P("dp", "seq", None), P())
    return jax.shard_map(
        per_device, mesh=mesh, in_specs=placed, out_specs=P("dp", "seq", None), check_vma=False
    )
```

profile of v0, /device:TPU:6, one launch (start us, length us, event | category | flops | bytes accessed | tf_op | source)
XLA Modules:
  0.0 457.0 jit_solution(14364019412051347033)
XLA Ops:
  0.0 1.5 copy.31
  1.5 1.6 copy.22
  3.2 18.8 %all-to-all-start = ((bf16[64,64,1,128]{3,0,2,1:T(8,128)(2,1)}), bf16[64,64,1,128]{3,0,2,1:T(8,128)(2,1)S(1)}, u32[]{:S(2)}, u32[]{:S(2)}) async-start(bf16[64,64,1,128]{3,0,2,1:T(8,128)(2,1)} %copy.22), calls=%async_computation | async-start | bytes 2097152 | tf_op jit(solution)/shard_map/all_to_all | solution.py:99
  22.1 53.7 %all-to-all-done = bf16[64,64,1,128]{3,0,2,1:T(8,128)(2,1)S(1)} async-done(((bf16[64,64,1,128]{3,0,2,1:T(8,128)(2,1)}), bf16[64,64,1,128]{3,0,2,1:T(8,128)(2,1)S(1)}, u32[]{:S(2)}, u32[]{:S(2)}) %all-to-all-start) | async-done | bytes 1048608 | tf_op jit(solution)/shard_map/all_to_all | solution.py:99
  77.0 6.9 %all-to-all-start.1 = ((bf16[64,64,1,128]{3,0,2,1:T(8,128)(2,1)}), bf16[64,64,1,128]{3,0,2,1:T(8,128)(2,1)S(1)}, u32[]{:S(2)}, u32[]{:S(2)}) async-start(bf16[64,64,1,128]{3,0,2,1:T(8,128)(2,1)} %bitcast.9), calls=%async_computation.1 | async-start | bytes 2097152 | tf_op jit(solution)/shard_map/all_to_all | solution.py:100
  83.9 53.5 %all-to-all-done.1 = bf16[64,64,1,128]{3,0,2,1:T(8,128)(2,1)S(1)} async-done(((bf16[64,64,1,128]{3,0,2,1:T(8,128)(2,1)}), bf16[64,64,1,128]{3,0,2,1:T(8,128)(2,1)S(1)}, u32[]{:S(2)}, u32[]{:S(2)}) %all-to-all-start.1) | async-done | bytes 1048608 | tf_op jit(solution)/shard_map/all_to_all | solution.py:100
  138.7 6.9 %all-to-all-start.2 = ((bf16[64,64,1,128]{3,0,2,1:T(8,128)(2,1)}), bf16[64,64,1,128]{3,0,2,1:T(8,128)(2,1)S(1)}, u32[]{:S(2)}, u32[]{:S(2)}) async-start(bf16[64,64,1,128]{3,0,2,1:T(8,128)(2,1)} %bitcast.13), calls=%async_computation.2 | async-start | bytes 2097152 | tf_op jit(solution)/shard_map/all_to_all | solution.py:101
  146.3 52.9 %all-to-all-done.2 = bf16[64,64,1,128]{3,0,2,1:T(8,128)(2,1)S(1)} async-done(((bf16[64,64,1,128]{3,0,2,1:T(8,128)(2,1)}), bf16[64,64,1,128]{3,0,2,1:T(8,128)(2,1)S(1)}, u32[]{:S(2)}, u32[]{:S(2)}) %all-to-all-start.2) | async-done | bytes 1048608 | tf_op jit(solution)/shard_map/all_to_all | solution.py:101
  199.7 191.6 %while.90 = (s32[]{:T(128)}, bf16[8,512,1,128]{3,1,0,2:T(8,128)(2,1)S(1)}, s32[129]{0:T(256)}, s32[8]{0:T(128)}, bf16[4096,1,128]{2,0,1:T(8,128)(2,1)S(1)}, /*in...) while((s32[]{:T(128)}, ...), condition=%wide.region_11.12_spmd, body=%wide.region_0.11_spmd.sunk | while | flops 103058992 | bytes 3005705 | solution.py:83
  203.5 1.4 reduce_min.17
  207.4 2.4 while.91
  209.9 3.0 while.92
  216.8 1.4 reduce_min.17
  220.8 4.7 %while.91 = (s32[]{:T(128)}, f32[1,512]{1,0:T(1,128)S(1)}, s32[]{:T(128)}, s32[512]{0:T(512)}, bf16[4096,1,128]{2,0,1:T(8,128)(2,1)}, /*index=5*/bf16[512,1,128]...) while((s32[]{:T(128)}, f32[1,512]{1,0:T(1,128)S(1)}, ...), condition=%wide.region_7.7_spmd.clone, body=%wide.region_5.6_spmd.clone.sunk | while | flops 34341636 | bytes 213159 | solution.py:52
  225.6 5.9 %while.92 = (s32[]{:T(128)}, f32[1,512]{1,0:T(1,128)S(1)}, f32[512,1,128]{0,2,1:T(8,128)S(1)}, s32[]{:T(128)}, s32[512]{0:T(512)}, /*index=5*/bf16[4096,1,128]{2...) while((s32[]{:T(128)}, f32[1,512]{1,0:T(1,128)S(1)}, ...), condition=%wide.region_10.10_spmd.clone, body=%wide.region_8.9_spmd.clone.sunk | while | flops 68354816 | bytes 1329347 | solution.py:72
  235.5 1.4 reduce_min.17
  239.4 7.1 %while.91 = (s32[]{:T(128)}, f32[1,512]{1,0:T(1,128)S(1)}, s32[]{:T(128)}, s32[512]{0:T(512)}, bf16[4096,1,128]{2,0,1:T(8,128)(2,1)}, /*index=5*/bf16[512,1,128]...) while((s32[]{:T(128)}, f32[1,512]{1,0:T(1,128)S(1)}, ...), condition=%wide.region_7.7_spmd.clone, body=%wide.region_5.6_spmd.clone.sunk | while | flops 34341636 | bytes 213159 | solution.py:52
  246.6 8.9 %while.92 = (s32[]{:T(128)}, f32[1,512]{1,0:T(1,128)S(1)}, f32[512,1,128]{0,2,1:T(8,128)S(1)}, s32[]{:T(128)}, s32[512]{0:T(512)}, /*index=5*/bf16[4096,1,128]{2...) while((s32[]{:T(128)}, f32[1,512]{1,0:T(1,128)S(1)}, ...), condition=%wide.region_10.10_spmd.clone, body=%wide.region_8.9_spmd.clone.sunk | while | flops 68354816 | bytes 1329347 | solution.py:72
  259.4 1.4 reduce_min.17
  263.4 9.4 %while.91 = (s32[]{:T(128)}, f32[1,512]{1,0:T(1,128)S(1)}, s32[]{:T(128)}, s32[512]{0:T(512)}, bf16[4096,1,128]{2,0,1:T(8,128)(2,1)}, /*index=5*/bf16[512,1,128]...) while((s32[]{:T(128)}, f32[1,512]{1,0:T(1,128)S(1)}, ...), condition=%wide.region_7.7_spmd.clone, body=%wide.region_5.6_spmd.clone.sunk | while | flops 34341636 | bytes 213159 | solution.py:52
  272.9 11.8 %while.92 = (s32[]{:T(128)}, f32[1,512]{1,0:T(1,128)S(1)}, f32[512,1,128]{0,2,1:T(8,128)S(1)}, s32[]{:T(128)}, s32[512]{0:T(512)}, /*index=5*/bf16[4096,1,128]{2...) while((s32[]{:T(128)}, f32[1,512]{1,0:T(1,128)S(1)}, ...), condition=%wide.region_10.10_spmd.clone, body=%wide.region_8.9_spmd.clone.sunk | while | flops 68354816 | bytes 1329347 | solution.py:72
  292.7 11.8 %while.91 = (s32[]{:T(128)}, f32[1,512]{1,0:T(1,128)S(1)}, s32[]{:T(128)}, s32[512]{0:T(512)}, bf16[4096,1,128]{2,0,1:T(8,128)(2,1)}, /*index=5*/bf16[512,1,128]...) while((s32[]{:T(128)}, f32[1,512]{1,0:T(1,128)S(1)}, ...), condition=%wide.region_7.7_spmd.clone, body=%wide.region_5.6_spmd.clone.sunk | while | flops 34341636 | bytes 213159 | solution.py:52
  304.5 14.8 %while.92 = (s32[]{:T(128)}, f32[1,512]{1,0:T(1,128)S(1)}, f32[512,1,128]{0,2,1:T(8,128)S(1)}, s32[]{:T(128)}, s32[512]{0:T(512)}, /*index=5*/bf16[4096,1,128]{2...) while((s32[]{:T(128)}, f32[1,512]{1,0:T(1,128)S(1)}, ...), condition=%wide.region_10.10_spmd.clone, body=%wide.region_8.9_spmd.clone.sunk | while | flops 68354816 | bytes 1329347 | solution.py:72
  323.3 1.4 reduce_min.17
  327.2 4.7 %while.91 = (s32[]{:T(128)}, f32[1,512]{1,0:T(1,128)S(1)}, s32[]{:T(128)}, s32[512]{0:T(512)}, bf16[4096,1,128]{2,0,1:T(8,128)(2,1)}, /*index=5*/bf16[512,1,128]...) while((s32[]{:T(128)}, f32[1,512]{1,0:T(1,128)S(1)}, ...), condition=%wide.region_7.7_spmd.clone, body=%wide.region_5.6_spmd.clone.sunk | while | flops 34341636 | bytes 213159 | solution.py:52
  332.0 5.9 %while.92 = (s32[]{:T(128)}, f32[1,512]{1,0:T(1,128)S(1)}, f32[512,1,128]{0,2,1:T(8,128)S(1)}, s32[]{:T(128)}, s32[512]{0:T(512)}, /*index=5*/bf16[4096,1,128]{2...) while((s32[]{:T(128)}, f32[1,512]{1,0:T(1,128)S(1)}, ...), condition=%wide.region_10.10_spmd.clone, body=%wide.region_8.9_spmd.clone.sunk | while | flops 68354816 | bytes 1329347 | solution.py:72
  345.9 7.1 %while.91 = (s32[]{:T(128)}, f32[1,512]{1,0:T(1,128)S(1)}, s32[]{:T(128)}, s32[512]{0:T(512)}, bf16[4096,1,128]{2,0,1:T(8,128)(2,1)}, /*index=5*/bf16[512,1,128]...) while((s32[]{:T(128)}, f32[1,512]{1,0:T(1,128)S(1)}, ...), condition=%wide.region_7.7_spmd.clone, body=%wide.region_5.6_spmd.clone.sunk | while | flops 34341636 | bytes 213159 | solution.py:52
  353.0 8.9 %while.92 = (s32[]{:T(128)}, f32[1,512]{1,0:T(1,128)S(1)}, f32[512,1,128]{0,2,1:T(8,128)S(1)}, s32[]{:T(128)}, s32[512]{0:T(512)}, /*index=5*/bf16[4096,1,128]{2...) while((s32[]{:T(128)}, f32[1,512]{1,0:T(1,128)S(1)}, ...), condition=%wide.region_10.10_spmd.clone, body=%wide.region_8.9_spmd.clone.sunk | while | flops 68354816 | bytes 1329347 | solution.py:72
  369.8 9.4 %while.91 = (s32[]{:T(128)}, f32[1,512]{1,0:T(1,128)S(1)}, s32[]{:T(128)}, s32[512]{0:T(512)}, bf16[4096,1,128]{2,0,1:T(8,128)(2,1)}, /*index=5*/bf16[512,1,128]...) while((s32[]{:T(128)}, f32[1,512]{1,0:T(1,128)S(1)}, ...), condition=%wide.region_7.7_spmd.clone, body=%wide.region_5.6_spmd.clone.sunk | while | flops 34341636 | bytes 213159 | solution.py:52
  379.3 11.8 %while.92 = (s32[]{:T(128)}, f32[1,512]{1,0:T(1,128)S(1)}, f32[512,1,128]{0,2,1:T(8,128)S(1)}, s32[]{:T(128)}, s32[512]{0:T(512)}, /*index=5*/bf16[4096,1,128]{2...) while((s32[]{:T(128)}, f32[1,512]{1,0:T(1,128)S(1)}, ...), condition=%wide.region_10.10_spmd.clone, body=%wide.region_8.9_spmd.clone.sunk | while | flops 68354816 | bytes 1329347 | solution.py:72
  391.9 1.4 reduce.6
  393.6 60.2 %all_to_all.60 = bf16[64,2,4096]{2,1,0:T(2,128)(2,1)S(1)} all-to-all(bf16[64,2,4096]{2,1,0:T(2,128)(2,1)S(1)} %reshape.134), channel_id=1, replica_groups=mesh['dp'=8,'seq'=64] {'seq'}, dimensions={0} | all-to-all | bytes 2097152 | tf_op jit(solution)/shard_map/all_to_all | solution.py:119
  (586 shorter events, 161.9 us)
Async XLA Ops:
  0.0 145.7 %copy-start = (s32[8,129]{1,0:T(8,128)S(1)}, s32[8,129]{1,0:T(8,128)}, u32[]{:S(2)}) copy-start(s32[8,129]{1,0:T(8,128)} %param.13) | copy-start | bytes 12388
  1.5 20.5 %copy-start.2 = (bf16[1,64,1024]{2,1,0:T(8,128)(2,1)S(1)}, bf16[1,64,1024]{2,1,0:T(8,128)(2,1)}, u32[]{:S(2)}) copy-start(bf16[1,64,1024]{2,1,0:T(8,128)(2,1)} %param.11) | copy-start | bytes 393220
  3.2 72.6 %all-to-all-start = ((bf16[64,64,1,128]{3,0,2,1:T(8,128)(2,1)}), bf16[64,64,1,128]{3,0,2,1:T(8,128)(2,1)S(1)}, u32[]{:S(2)}, u32[]{:S(2)}) async-start(bf16[64,64,1,128]{3,0,2,1:T(8,128)(2,1)} %copy.22), calls=%async_computation | async-start | bytes 2097152 | tf_op jit(solution)/shard_map/all_to_all | solution.py:99
  22.0 61.9 %copy-start.3 = (bf16[1,64,1024]{2,1,0:T(8,128)(2,1)S(1)}, bf16[1,64,1024]{2,1,0:T(8,128)(2,1)}, u32[]{:S(2)}) copy-start(bf16[1,64,1024]{2,1,0:T(8,128)(2,1)} %param.12) | copy-start | bytes 393220
  77.0 60.4 %all-to-all-start.1 = ((bf16[64,64,1,128]{3,0,2,1:T(8,128)(2,1)}), bf16[64,64,1,128]{3,0,2,1:T(8,128)(2,1)S(1)}, u32[]{:S(2)}, u32[]{:S(2)}) async-start(bf16[64,64,1,128]{3,0,2,1:T(8,128)(2,1)} %bitcast.9), calls=%async_computation.1 | async-start | bytes 2097152 | tf_op jit(solution)/shard_map/all_to_all | solution.py:100
  137.4 1.3 copy-start.1
  138.7 60.4 %all-to-all-start.2 = ((bf16[64,64,1,128]{3,0,2,1:T(8,128)(2,1)}), bf16[64,64,1,128]{3,0,2,1:T(8,128)(2,1)S(1)}, u32[]{:S(2)}, u32[]{:S(2)}) async-start(bf16[64,64,1,128]{3,0,2,1:T(8,128)(2,1)} %bitcast.13), calls=%async_computation.2 | async-start | bytes 2097152 | tf_op jit(solution)/shard_map/all_to_all | solution.py:101
where the time goes:
time: 463 us; the launch traced here: 457 us
  waiting for transfers between devices  160 us (35%)
  matrix products  121 us (26%)
  blocking collectives  60.2 us (13%)
  starting transfers between devices  32.5 us (7%)
  loops' own time  30.5 us (7%)
  local copies, waits for them, and re-layouts  28.7 us (6%)
  other arithmetic  23.7 us (5%)
    dot_general x96, matrix products, tile(): jnp.einsum('qhd,thd->hqt', query_block, key_tile, preferred_element_type=...  110 us
    all_to_all x1, blocking collectives, per_device(): lax.all_to_all(result, 'seq', split_axis=0, concat_axis=1, tiled=True)  60.2 us
    all_to_all x1, waiting for transfers between devices, per_device(): lax.all_to_all(query_split, 'seq', split_axis=1, concat_axis=0, tiled=True)  53.7 us
    all_to_all x1, waiting for transfers between devices, per_device(): lax.all_to_all(key_split, 'seq', split_axis=1, concat_axis=0, tiled=True)  53.5 us
    all_to_all x1, waiting for transfers between devices, per_device(): lax.all_to_all(value_split, 'seq', split_axis=1, concat_axis=0, tiled=True)  52.9 us
    another operation x1, loops' own time, attend_blocks(): return lax.map(one_block, block_list)  25.9 us
    all_to_all x1, starting transfers between devices, per_device(): lax.all_to_all(query_split, 'seq', split_axis=1, concat_axis=0, tiled=True)  18.8 us
    reduce_min x8, other arithmetic, one_block(): first_block = jnp.min(starts) // key_rows  11.1 us
  transfers between devices with their start and end apart: 3, of which 3 were waited for; matrix products, arithmetic and copies ran while one was open for 0% of the time, Pallas kernels for 0%

commit v1 on v0

v1 whole, which is shorter than its diff:
```python
import functools
import math

import jax
import jax.numpy as jnp
from jax import lax
from jax.experimental import pallas as pl
from jax.experimental.pallas import tpu as pltpu
from jax.sharding import PartitionSpec as P

QH = 64
KVH = 8
HD = 128
GROUP = 8
XN = 4
NEG = -1e30
MESH = pl.DeviceIdType.MESH


def kernel(
    zn, tok, q_ref, k_ref, v_ref, len_ref, o_ref,
    qbuf, kvbuf, obuf, acc, mx, sm, starts,
    kv_ssem, kv_rsem, kv_lsem, q_ssem, q_rsem, q_lsem,
    rt_ssem, rt_rsem, lf_ssem, lf_rsem, o_ssem, o_rsem, o_lsem,
):
    me = lax.axis_index("seq")
    x, z = me // zn, me % zn
    dp = lax.axis_index("dp")
    up = x * zn + (z + 1) % zn
    down = x * zn + (z + zn - 1) % zn
    scale2 = math.log2(math.e) / math.sqrt(HD)
    half_ring = zn // 2
    kvw = GROUP * HD

    def peer(d):
        return (x + d) % XN

    barrier = pltpu.get_barrier_semaphore()
    for other in [up, down] + [peer(d) * zn + z for d in range(1, XN)]:
        pl.semaphore_signal(barrier, inc=1, device_id={"seq": other}, device_id_type=MESH)
    pl.semaphore_wait(barrier, XN + 1)

    def kv_copy(d, h, which):
        src = (k_ref, v_ref)[which]
        to = peer(d)
        lane = pl.multiple_of((to * 2 + h) * HD, HD)
        return pltpu.make_async_remote_copy(
            src_ref=src.at[0, :, pl.ds(lane, HD)],
            dst_ref=kvbuf.at[h, x // 2, z, which, x % 2],
            send_sem=kv_ssem.at[d - 1, h, which],
            recv_sem=kv_rsem.at[d - 1, h, which],
            device_id={"seq": to * zn + z},
            device_id_type=MESH,
        )

    def kv_own(h, which):
        src = (k_ref, v_ref)[which]
        lane = pl.multiple_of((x * 2 + h) * HD, HD)
        return pltpu.make_async_copy(
            src.at[0, :, pl.ds(lane, HD)],
            kvbuf.at[h, x // 2, z, which, x % 2],
            kv_lsem.at[h, which],
        )

    def q_copy(d, h):
        to = peer(d)
        lane = pl.multiple_of((to * 2 + h) * kvw, kvw)
        return pltpu.make_async_remote_copy(
            src_ref=q_ref.at[0, :, pl.ds(lane, kvw)],
            dst_ref=qbuf.at[h, x],
            send_sem=q_ssem.at[d - 1, h],
            recv_sem=q_rsem.at[d - 1, h],
            device_id={"seq": to * zn + z},
            device_id_type=MESH,
        )

    def q_own(h):
        lane = pl.multiple_of((x * 2 + h) * kvw, kvw)
        return pltpu.make_async_copy(
            q_ref.at[0, :, pl.ds(lane, kvw)], qbuf.at[h, x], q_lsem.at[h]
        )

    def o_copy(d, h):
        to = peer(d)
        lane = pl.multiple_of((x * 2 + h) * kvw, kvw)
        return pltpu.make_async_remote_copy(
            src_ref=obuf.at[h, to],
            dst_ref=o_ref.at[0, :, pl.ds(lane, kvw)],
            send_sem=o_ssem.at[d - 1, h],
            recv_sem=o_rsem.at[d - 1, h],
            device_id={"seq": to * zn + z},
            device_id_type=MESH,
        )

    def o_own(h):
        lane = pl.multiple_of((x * 2 + h) * kvw, kvw)
        return pltpu.make_async_copy(
            obuf.at[h, x], o_ref.at[0, :, pl.ds(lane, kvw)], o_lsem.at[h]
        )

    def right(h, half, s):
        block = kvbuf.at[h, half, (z + zn - s) % zn]
        return pltpu.make_async_remote_copy(
            src_ref=block, dst_ref=block,
            send_sem=rt_ssem.at[h, half, s], recv_sem=rt_rsem.at[h, half, s],
            device_id={"seq": up}, device_id_type=MESH,
        )

    def left(h, half, s):
        block = kvbuf.at[h, half, (z + s) % zn]
        return pltpu.make_async_remote_copy(
            src_ref=block, dst_ref=block,
            send_sem=lf_ssem.at[h, half, s], recv_sem=lf_rsem.at[h, half, s],
            device_id={"seq": down}, device_id_type=MESH,
        )

    for h in range(2):
        for d in range(1, XN):
            for which in range(2):
                kv_copy(d, h, which).start()
        for which in range(2):
            kv_own(h, which).start()
    for h in range(2):
        for d in range(1, XN):
            q_copy(d, h).start()
        q_own(h).start()

    def start_ring(h):
        for d in range(1, XN):
            for which in range(2):
                kv_copy(d, h, which).wait_recv()
        for which in range(2):
            kv_own(h, which).wait()
        for half in range(2):
            right(h, half, 0).start()
            left(h, half, 0).start()

    def wait_queries(h):
        for d in range(1, XN):
            q_copy(d, h).wait_recv()
        q_own(h).wait()

    lengths = len_ref[pl.ds(dp, 1), :].astype(jnp.float32)
    docs = lengths.shape[1]
    before = (
        lax.broadcasted_iota(jnp.int32, (docs, docs), 0)
        <= lax.broadcasted_iota(jnp.int32, (docs, docs), 1)
    ).astype(jnp.float32)
    ends = lax.dot_general(
        jnp.broadcast_to(lengths, (8, docs)), before, (((1,), (0,)), ((), ())),
        precision=lax.Precision.HIGHEST, preferred_element_type=jnp.float32,
    )[0:1, :]
    ends = jnp.broadcast_to(ends, (tok, docs))

    def first_position(r):
        return (r * zn + z) * tok

    def find_starts():
        for r in range(XN):
            positions = (
                first_position(r) + lax.broadcasted_iota(jnp.int32, (tok, docs), 0)
            ).astype(jnp.float32)
            first = jnp.max(jnp.where(ends <= positions, ends, 0.0), axis=1, keepdims=True)
            starts[r] = jnp.broadcast_to(first.astype(jnp.int32), (tok, HD))

    def bias_of(r, blocks):
        q_pos = first_position(r) + lax.broadcasted_iota(jnp.int32, (tok, HD), 0)
        first = starts[r]
        lane = lax.broadcasted_iota(jnp.int32, (tok, HD), 1)
        parts = []
        for i in range(0, len(blocks), 2):
            (ra, za), (rb, zb) = blocks[i], blocks[i + 1]
            base_a, base_b = (ra * zn + za) * tok, (rb * zn + zb) * tok - tok
            k_pos = jnp.where(lane < tok, base_a, base_b) + lane
            ok = (k_pos >= first) & (k_pos <= q_pos)
            parts.append(jnp.where(ok, 0.0, NEG).astype(jnp.float32))
        return parts

    heads_tile = 4

    def update(h, half, r, zs, only_first, fresh):
        rows = [0] if only_first else [0, 1]
        blocks = [(2 * half + k, zb) for zb in zs for k in rows]
        bias = bias_of(r, blocks)
        keys = jnp.concatenate([kvbuf[h, half, zb, 0, k] for zb in zs for k in rows], axis=0)
        vals = jnp.concatenate([kvbuf[h, half, zb, 1, k] for zb in zs for k in rows], axis=0)
        groups = len(bias)
        rows_tile = heads_tile * tok

        def tile(j, carry):
            lanes = pl.multiple_of(j * heads_tile * HD, heads_tile * HD)
            at = pl.ds(pl.multiple_of(j * rows_tile, rows_tile), rows_tile)
            q = qbuf[h, r, :, pl.ds(lanes, heads_tile * HD)]
            q = jnp.concatenate([q[:, i * HD:(i + 1) * HD] for i in range(heads_tile)], axis=0)
            s = lax.dot_general(
                q, keys, (((1,), (1,)), ((), ())), preferred_element_type=jnp.float32
            )
            parts = [
                (s[:, g * HD:(g + 1) * HD].reshape(heads_tile, tok, HD) * scale2 + bias[g][None])
                .reshape(rows_tile, HD)
                for g in range(groups)
            ]
            top = functools.reduce(jnp.maximum, parts)
            top = jnp.max(top, axis=1, keepdims=True)
            if fresh:
                m_new = jnp.broadcast_to(top, (rows_tile, HD))
            else:
                m_old = mx[r, at, :]
                m_new = jnp.maximum(m_old, top)
            w = [jnp.exp2(p - m_new).astype(jnp.bfloat16) for p in parts]
            part_sum = functools.reduce(jnp.add, [p.astype(jnp.float32) for p in w])
            prod = jnp.dot(
                jnp.concatenate(w, axis=1), vals, preferred_element_type=jnp.float32
            )
            if fresh:
                acc[r, at, :] = prod
                sm[r, at, :] = part_sum
            else:
                alpha = jnp.exp2(m_old - m_new)
                acc[r, at, :] = acc[r, at, :] * alpha + prod
                sm[r, at, :] = sm[r, at, :] * alpha + part_sum
            mx[r, at, :] = m_new
            return carry

        lax.fori_loop(0, GROUP // heads_tile, tile, 0)

    def work(h, half, zs, seen, fresh=False):
        update(h, half, 2 * half + 1, zs, False, fresh)
        single = len(zs) == 1

        if seen is None:
            update(h, half, 2 * half, zs, not single, fresh)
        else:
            @pl.when(seen)
            def _():
                update(h, half, 2 * half, zs, not single, fresh)
        if half == 0:
            @pl.when(z == 0)
            def _():
                update(h, 0, 2, zs, False, False)

    def finish(h):
        for d in (2, 1, 3, 0):
            r = peer(d)
            for i in range(GROUP):
                at = pl.ds(i * tok, tok)
                total = jnp.sum(sm[r, at, :], axis=1, keepdims=True)
                obuf[h, r, :, i * HD:(i + 1) * HD] = (acc[r, at, :] / total).astype(jnp.bfloat16)
            if d:
                o_copy(d, h).start()
            else:
                o_own(h).start()

    right_steps = (half_ring, half_ring - 1)
    left_steps = (half_ring - 1, half_ring)

    def forward_pair(h, s):
        for half in range(2):
            right(h, half, s - 1).wait_recv()
            if right_steps[half] == half_ring:
                right(h, half, s).start()
            else:
                @pl.when(s < half_ring - 1)
                def _():
                    right(h, half, s).start()
            left(h, half, s - 1).wait_recv()
            if left_steps[half] == half_ring:
                left(h, half, s).start()
            else:
                @pl.when(s < half_ring - 1)
                def _():
                    left(h, half, s).start()

    def work_pair(h, s):
        zs = [(z + zn - s) % zn, (z + s) % zn]
        seen = (z >= s) | (z + s >= zn)
        for half in (1, 0):
            work(h, half, zs, seen)

    start_ring(0)
    find_starts()
    for h in range(2):
        if h == 0:
            forward_pair(h, 1)
            wait_queries(h)
        else:
            wait_queries(h)
        for half in (1, 0):
            work(h, half, [z], None, fresh=True)
        if h == 1:
            forward_pair(h, 1)
        work_pair(h, 1)

        def step(s, carry):
            forward_pair(h, s)
            work_pair(h, s)
            return carry

        lax.fori_loop(2, half_ring, step, 0)
        if h == 0:
            start_ring(1)
        right(h, 0, half_ring - 1).wait_recv()
        left(h, 1, half_ring - 1).wait_recv()
        far = (z + half_ring) % zn
        for half in (1, 0):
            work(h, half, [far], z >= half_ring)
        finish(h)

    for h in range(2):
        for d in range(1, XN):
            o_copy(d, h).wait()
            q_copy(d, h).wait_send()
            for which in range(2):
                kv_copy(d, h, which).wait_send()
        o_own(h).wait()
        for half in range(2):
            def drain_right(s, carry):
                right(h, half, s).wait_send()
                return carry

            def drain_left(s, carry):
                left(h, half, s).wait_send()
                return carry

            lax.fori_loop(0, right_steps[half], drain_right, 0)
            lax.fori_loop(0, left_steps[half], drain_left, 0)


def per_device(queries, keys, values, doc_lengths):
    tok = queries.shape[1]
    zn = lax.axis_size("seq") // XN
    dma, vmem = pltpu.SemaphoreType.DMA, pltpu.VMEM
    kvw = GROUP * HD
    return pl.pallas_call(
        functools.partial(kernel, zn, tok),
        out_shape=jax.ShapeDtypeStruct(queries.shape, jnp.bfloat16),
        in_specs=[pl.BlockSpec(memory_space=pltpu.VMEM)] * 4,
        out_specs=pl.BlockSpec(memory_space=pltpu.VMEM),
        scratch_shapes=[
            vmem((2, XN, tok, kvw), jnp.bfloat16),
            vmem((2, 2, zn, 2, 2, tok, HD), jnp.bfloat16),
            vmem((2, XN, tok, kvw), jnp.bfloat16),
            vmem((XN, GROUP * tok, HD), jnp.float32),
            vmem((XN, GROUP * tok, HD), jnp.float32),
            vmem((XN, GROUP * tok, HD), jnp.float32),
            vmem((XN, tok, HD), jnp.int32),
            dma((XN - 1, 2, 2)), dma((XN - 1, 2, 2)), dma((2, 2)),
            dma((XN - 1, 2)), dma((XN - 1, 2)), dma((2,)),
            dma((2, 2, zn // 2)), dma((2, 2, zn // 2)),
            dma((2, 2, zn // 2)), dma((2, 2, zn // 2)),
            dma((XN - 1, 2)), dma((XN - 1, 2)), dma((2,)),
        ],
        compiler_params=pltpu.CompilerParams(collective_id=0, has_side_effects=True),
        name="ring_attention",
    )(queries, keys, values, doc_lengths)


def solution(mesh):
    placed = (P("dp", "seq", None), P("dp", "seq", None), P("dp", "seq", None), P())
    return jax.shard_map(
        per_device, mesh=mesh, in_specs=placed, out_specs=P("dp", "seq", None), check_vma=False
    )
```

time: 463 us -> 107 us (0.23)
  the two profiles are of different devices: /device:TPU:6 before, /device:TPU:24 now
where the time goes in v1:
time: 107 us
  Pallas kernels  105 us (98%)
  local copies, waits for them, and re-layouts  2.26 us (2%)
    pallas_call x1, Pallas kernels, per_device(): pl.pallas_call(functools.partial(kernel, zn, tok), out_shape=jax.ShapeDty...  105 us
    unnamed x1, local copies, waits for them, and re-layouts  2.26 us

profile of v1, /device:TPU:24, one launch (start us, length us, event | category | flops | bytes accessed | tf_op | source)
XLA Modules:
  0.0 107.0 jit_solution(12064534922412486776)
XLA Ops:
  0.0 104.8 %ring_attention.1 = bf16[1,64,8192]{2,1,0:T(8,128)(2,1)} custom-call(bf16[1,64,8192]{2,1,0:T(8,128)(2,1)} %q_ref.1, bf16[1,64,1024]{2,1,0:T(8,128)(2,1)} %k_ref.1, bf16[1,64,1024]{2,1,0:T(8,128)(2,1)} %v_ref.1, s32[8,129]{1,0:T(8,128)} %len_ref.1), custom_call_target="tpu_custom_call" | custom-call | tf_op jit(solution)/shard_map/ring_attention/pallas_call | solution.py:334
  104.8 2.3 %copy.6 = bf16[1,64,8192]{2,1,0:T(8,128)(2,1)} copy(bf16[1,64,8192]{2,1,0:T(8,128)(2,1)} %ring_attention.1) | data formatting | bytes 2097152

commit v2 on v1

--- a/solution.py
+++ b/solution.py
@@ -14,12 +14,13 @@
 GROUP = 8
 XN = 4
 NEG = -1e30
+SUMS = 16
 MESH = pl.DeviceIdType.MESH
 
 
 def kernel(
     zn, tok, q_ref, k_ref, v_ref, len_ref, o_ref,
-    qbuf, kvbuf, obuf, acc, mx, sm, starts,
+    qbuf, kvbuf, obuf, acc, mx, starts,
     kv_ssem, kv_rsem, kv_lsem, q_ssem, q_rsem, q_lsem,
     rt_ssem, rt_rsem, lf_ssem, lf_rsem, o_ssem, o_rsem, o_lsem,
 ):
@@ -143,86 +144,64 @@
     lengths = len_ref[pl.ds(dp, 1), :].astype(jnp.float32)
     docs = lengths.shape[1]
     before = (
-        lax.broadcasted_iota(jnp.int32, (docs, docs), 0)
-        <= lax.broadcasted_iota(jnp.int32, (docs, docs), 1)
+        lax.broadcasted_iota(jnp.int32, (docs, docs), 1)
+        <= lax.broadcasted_iota(jnp.int32, (docs, docs), 0)
     ).astype(jnp.float32)
-    ends = lax.dot_general(
-        jnp.broadcast_to(lengths, (8, docs)), before, (((1,), (0,)), ((), ())),
-        precision=lax.Precision.HIGHEST, preferred_element_type=jnp.float32,
-    )[0:1, :]
-    ends = jnp.broadcast_to(ends, (tok, docs))
 
     def first_position(r):
         return (r * zn + z) * tok
 
+    def token_row(rows):
+        lane = lax.broadcasted_iota(jnp.int32, (rows, 2 * tok), 1)
+        return jnp.where(lane < tok, lane, lane - tok)
+
     def find_starts():
+        ends = jnp.sum(before * lengths, axis=1, keepdims=True)
+        ends = jnp.broadcast_to(ends, (docs, 2 * tok))
         for r in range(XN):
-            positions = (
-                first_position(r) + lax.broadcasted_iota(jnp.int32, (tok, docs), 0)
-            ).astype(jnp.float32)
-            first = jnp.max(jnp.where(ends <= positions, ends, 0.0), axis=1, keepdims=True)
-            starts[r] = jnp.broadcast_to(first.astype(jnp.int32), (tok, HD))
+            positions = (first_position(r) + token_row(docs)).astype(jnp.float32)
+            first = jnp.max(jnp.where(ends <= positions, ends, 0.0), axis=0, keepdims=True)
+            starts[r] = jnp.broadcast_to(first.astype(jnp.int32), (8, 2 * tok))
 
     def bias_of(r, blocks):
-        q_pos = first_position(r) + lax.broadcasted_iota(jnp.int32, (tok, HD), 0)
-        first = starts[r]
-        lane = lax.broadcasted_iota(jnp.int32, (tok, HD), 1)
+        q_pos = first_position(r) + token_row(tok)
+        first = jnp.broadcast_to(starts[r][0:1, :], (tok, 2 * tok))
+        key = lax.broadcasted_iota(jnp.int32, (tok, 2 * tok), 0)
         parts = []
-        for i in range(0, len(blocks), 2):
-            (ra, za), (rb, zb) = blocks[i], blocks[i + 1]
-            base_a, base_b = (ra * zn + za) * tok, (rb * zn + zb) * tok - tok
-            k_pos = jnp.where(lane < tok, base_a, base_b) + lane
+        for rk, zk in blocks:
+            k_pos = (rk * zn + zk) * tok + key
             ok = (k_pos >= first) & (k_pos <= q_pos)
             parts.append(jnp.where(ok, 0.0, NEG).astype(jnp.float32))
-        return parts
+        return jnp.concatenate(parts, axis=0)
 
     heads_tile = 4
+    cols = heads_tile * tok
 
     def update(h, half, r, zs, only_first, fresh):
         rows = [0] if only_first else [0, 1]
-        blocks = [(2 * half + k, zb) for zb in zs for k in rows]
-        bias = bias_of(r, blocks)
+        bias = bias_of(r, [(2 * half + k, zb) for zb in zs for k in rows])
         keys = jnp.concatenate([kvbuf[h, half, zb, 0, k] for zb in zs for k in rows], axis=0)
         vals = jnp.concatenate([kvbuf[h, half, zb, 1, k] for zb in zs for k in rows], axis=0)
-        groups = len(bias)
-        rows_tile = heads_tile * tok
-
-        def tile(j, carry):
-            lanes = pl.multiple_of(j * heads_tile * HD, heads_tile * HD)
-            at = pl.ds(pl.multiple_of(j * rows_tile, rows_tile), rows_tile)
-            q = qbuf[h, r, :, pl.ds(lanes, heads_tile * HD)]
+        count = keys.shape[0]
+        vals = jnp.concatenate([vals.T, jnp.ones((SUMS, count), jnp.bfloat16)], axis=0)
+        for j in range(GROUP // heads_tile):
+            q = qbuf[h, r, :, j * heads_tile * HD:(j + 1) * heads_tile * HD]
             q = jnp.concatenate([q[:, i * HD:(i + 1) * HD] for i in range(heads_tile)], axis=0)
+            at = slice(j * cols, (j + 1) * cols)
             s = lax.dot_general(
-                q, keys, (((1,), (1,)), ((), ())), preferred_element_type=jnp.float32
+                keys, q, (((1,), (1,)), ((), ())), preferred_element_type=jnp.float32
             )
-            parts = [
-                (s[:, g * HD:(g + 1) * HD].reshape(heads_tile, tok, HD) * scale2 + bias[g][None])
-                .reshape(rows_tile, HD)
-                for g in range(groups)
-            ]
-            top = functools.reduce(jnp.maximum, parts)
-            top = jnp.max(top, axis=1, keepdims=True)
-            if fresh:
-                m_new = jnp.broadcast_to(top, (rows_tile, HD))
-            else:
-                m_old = mx[r, at, :]
-                m_new = jnp.maximum(m_old, top)
-            w = [jnp.exp2(p - m_new).astype(jnp.bfloat16) for p in parts]
-            part_sum = functools.reduce(jnp.add, [p.astype(jnp.float32) for p in w])
-            prod = jnp.dot(
-                jnp.concatenate(w, axis=1), vals, preferred_element_type=jnp.float32
-            )
-            if fresh:
-                acc[r, at, :] = prod
-                sm[r, at, :] = part_sum
-            else:
-                alpha = jnp.exp2(m_old - m_new)
-                acc[r, at, :] = acc[r, at, :] * alpha + prod
-                sm[r, at, :] = sm[r, at, :] * alpha + part_sum
-            mx[r, at, :] = m_new
-            return carry
-
-        lax.fori_loop(0, GROUP // heads_tile, tile, 0)
+            s = s * scale2 + jnp.concatenate([bias] * (heads_tile // 2), axis=1)
+            m_new = jnp.max(s, axis=0, keepdims=True)
+            if not fresh:
+                m_old = mx[h, r, 0:1, at]
+                m_new = jnp.maximum(m_old, m_new)
+            w = jnp.exp2(s - m_new).astype(jnp.bfloat16)
+            prod = jnp.dot(vals, w, preferred_element_type=jnp.float32)
+            if not fresh:
+                prod = acc[h, r, :, at] * jnp.exp2(m_old - m_new) + prod
+            acc[h, r, :, at] = prod
+            mx[h, r, 0:1, at] = m_new
 
     def work(h, half, zs, seen, fresh=False):
         update(h, half, 2 * half + 1, zs, False, fresh)
@@ -240,12 +219,15 @@
                 update(h, 0, 2, zs, False, False)
 
     def finish(h):
+        def one(r):
+            o = acc[h, r, :HD, :] / acc[h, r, HD:HD + 1, :]
+            for i in range(GROUP):
+                obuf[h, r, :, i * HD:(i + 1) * HD] = (
+                    o[:, i * tok:(i + 1) * tok].T.astype(jnp.bfloat16)
+                )
+
         for d in (2, 1, 3, 0):
-            r = peer(d)
-            for i in range(GROUP):
-                at = pl.ds(i * tok, tok)
-                total = jnp.sum(sm[r, at, :], axis=1, keepdims=True)
-                obuf[h, r, :, i * HD:(i + 1) * HD] = (acc[r, at, :] / total).astype(jnp.bfloat16)
+            one(peer(d))
             if d:
                 o_copy(d, h).start()
             else:
@@ -254,55 +236,54 @@
     right_steps = (half_ring, half_ring - 1)
     left_steps = (half_ring - 1, half_ring)
 
-    def forward_pair(h, s):
-        for half in range(2):
-            right(h, half, s - 1).wait_recv()
-            if right_steps[half] == half_ring:
-                right(h, half, s).start()
+    def forward(h, half, s):
+        for copy, steps in ((right, right_steps), (left, left_steps)):
+            copy(h, half, s - 1).wait_recv()
+            if steps[half] == half_ring:
+                copy(h, half, s).start()
             else:
                 @pl.when(s < half_ring - 1)
                 def _():
-                    right(h, half, s).start()
-            left(h, half, s - 1).wait_recv()
-            if left_steps[half] == half_ring:
-                left(h, half, s).start()
-            else:
-                @pl.when(s < half_ring - 1)
-                def _():
-                    left(h, half, s).start()
-
-    def work_pair(h, s):
-        zs = [(z + zn - s) % zn, (z + s) % zn]
-        seen = (z >= s) | (z + s >= zn)
+                    copy(h, half, s).start()
+
+    def over_heads(body):
+        lax.fori_loop(0, 2, lambda h, carry: (body(h), carry)[1], 0)
+
+    def work_pair(h, half, s):
+        work(h, half, [(z + zn - s) % zn, (z + s) % zn], (z >= s) | (z + s >= zn))
+
+    start_ring(0)
+    start_ring(1)
+    find_starts()
+    for h in range(2):
         for half in (1, 0):
-            work(h, half, zs, seen)
-
-    start_ring(0)
-    find_starts()
-    for h in range(2):
-        if h == 0:
-            forward_pair(h, 1)
-            wait_queries(h)
-        else:
-            wait_queries(h)
+            forward(h, half, 1)
+    for h in range(2):
+        wait_queries(h)
+
+    def first_step(h):
         for half in (1, 0):
             work(h, half, [z], None, fresh=True)
-        if h == 1:
-            forward_pair(h, 1)
-        work_pair(h, 1)
-
-        def step(s, carry):
-            forward_pair(h, s)
-            work_pair(h, s)
-            return carry
-
-        lax.fori_loop(2, half_ring, step, 0)
-        if h == 0:
-            start_ring(1)
-        right(h, 0, half_ring - 1).wait_recv()
-        left(h, 1, half_ring - 1).wait_recv()
-        far = (z + half_ring) % zn
         for half in (1, 0):
+            work_pair(h, half, 1)
+
+    over_heads(first_step)
+
+    def step(s, carry):
+        def heads(h):
+            for half in (1, 0):
+                forward(h, half, s)
+                work_pair(h, half, s)
+
+        over_heads(heads)
+        return carry
+
+    lax.fori_loop(2, half_ring, step, 0)
+    far = (z + half_ring) % zn
+
+    for h in range(2):
+        for half in (1, 0):
+            (right if half == 0 else left)(h, half, half_ring - 1).wait_recv()
             work(h, half, [far], z >= half_ring)
         finish(h)
 
@@ -340,10 +321,9 @@
             vmem((2, XN, tok, kvw), jnp.bfloat16),
             vmem((2, 2, zn, 2, 2, tok, HD), jnp.bfloat16),
             vmem((2, XN, tok, kvw), jnp.bfloat16),
-            vmem((XN, GROUP * tok, HD), jnp.float32),
-            vmem((XN, GROUP * tok, HD), jnp.float32),
-            vmem((XN, GROUP * tok, HD), jnp.float32),
-            vmem((XN, tok, HD), jnp.int32),
+            vmem((2, XN, HD + SUMS, GROUP * tok), jnp.float32),
+            vmem((2, XN, 8, GROUP * tok), jnp.float32),
+            vmem((XN, 8, 2 * tok), jnp.int32),
             dma((XN - 1, 2, 2)), dma((XN - 1, 2, 2)), dma((2, 2)),
             dma((XN - 1, 2)), dma((XN - 1, 2)), dma((2,)),
             dma((2, 2, zn // 2)), dma((2, 2, zn // 2)),

time: 107 us -> 88.9 us (0.83)
  Pallas kernels: 105 us -> 85.9 us
    pallas_call x1, Pallas kernels: 105 us -> 85.9 us  [per_device(): pl.pallas_call(functools.partial(kernel, zn, tok), out_shape=jax.ShapeDty...]
where the time goes in v2:
time: 88.9 us; the launch traced here: 88.2 us
  Pallas kernels  85.9 us (97%)
  local copies, waits for them, and re-layouts  2.26 us (3%)
    pallas_call x1, Pallas kernels, per_device(): pl.pallas_call(functools.partial(kernel, zn, tok), out_shape=jax.ShapeDty...  85.9 us
    unnamed x1, local copies, waits for them, and re-layouts  2.26 us

profile of v2, /device:TPU:24, one launch (start us, length us, event | category | flops | bytes accessed | tf_op | source)
XLA Modules:
  0.0 88.2 jit_solution(5153178597088410204)
XLA Ops:
  0.0 85.9 %ring_attention.1 = bf16[1,64,8192]{2,1,0:T(8,128)(2,1)} custom-call(bf16[1,64,8192]{2,1,0:T(8,128)(2,1)} %q_ref.1, bf16[1,64,1024]{2,1,0:T(8,128)(2,1)} %k_ref.1, bf16[1,64,1024]{2,1,0:T(8,128)(2,1)} %v_ref.1, s32[8,129]{1,0:T(8,128)} %len_ref.1), custom_call_target="tpu_custom_call" | custom-call | tf_op jit(solution)/shard_map/ring_attention/pallas_call | solution.py:315
  85.9 2.3 %copy.6 = bf16[1,64,8192]{2,1,0:T(8,128)(2,1)} copy(bf16[1,64,8192]{2,1,0:T(8,128)(2,1)} %ring_attention.1) | data formatting | bytes 2097152

commit v3 on v2

--- a/solution.py
+++ b/solution.py
@@ -121,11 +121,6 @@
                 kv_copy(d, h, which).start()
         for which in range(2):
             kv_own(h, which).start()
-    for h in range(2):
-        for d in range(1, XN):
-            q_copy(d, h).start()
-        q_own(h).start()
-
     def start_ring(h):
         for d in range(1, XN):
             for which in range(2):
@@ -177,46 +172,70 @@
     heads_tile = 4
     cols = heads_tile * tok
 
-    def update(h, half, r, zs, only_first, fresh):
-        rows = [0] if only_first else [0, 1]
-        bias = bias_of(r, [(2 * half + k, zb) for zb in zs for k in rows])
-        keys = jnp.concatenate([kvbuf[h, half, zb, 0, k] for zb in zs for k in rows], axis=0)
-        vals = jnp.concatenate([kvbuf[h, half, zb, 1, k] for zb in zs for k in rows], axis=0)
-        count = keys.shape[0]
-        vals = jnp.concatenate([vals.T, jnp.ones((SUMS, count), jnp.bfloat16)], axis=0)
-        for j in range(GROUP // heads_tile):
-            q = qbuf[h, r, :, j * heads_tile * HD:(j + 1) * heads_tile * HD]
+    def update(h, half, rows, zs, fresh):
+        order = [(k, zb) for k in range(2) for zb in zs]
+        keys = jnp.concatenate([kvbuf[h, half, zb, 0, k] for k, zb in order], axis=0)
+        vals = jnp.concatenate([kvbuf[h, half, zb, 1, k] for k, zb in order], axis=0)
+        vals = jnp.concatenate([vals.T, jnp.ones((SUMS, vals.shape[0]), jnp.bfloat16)], axis=0)
+        tiles = []
+        for r, only_first in rows:
+            blocks = order[:len(zs)] if only_first else order
+            bias = bias_of(r, [(2 * half + k, zb) for k, zb in blocks])
+            bias = jnp.concatenate([bias] * (heads_tile // 2), axis=1)
+            for j in range(GROUP // heads_tile):
+                tiles.append((r, bias, slice(j * cols, (j + 1) * cols), j * heads_tile * HD))
+
+        def score(tile):
+            r, bias, _, lane = tile
+            q = qbuf[h, r, :, lane:lane + heads_tile * HD]
             q = jnp.concatenate([q[:, i * HD:(i + 1) * HD] for i in range(heads_tile)], axis=0)
-            at = slice(j * cols, (j + 1) * cols)
-            s = lax.dot_general(
-                keys, q, (((1,), (1,)), ((), ())), preferred_element_type=jnp.float32
+            return lax.dot_general(
+                keys[:bias.shape[0]], q, (((1,), (1,)), ((), ())),
+                preferred_element_type=jnp.float32,
             )
-            s = s * scale2 + jnp.concatenate([bias] * (heads_tile // 2), axis=1)
-            m_new = jnp.max(s, axis=0, keepdims=True)
+
+        old = [None if fresh else mx[h, r, 0:1, at] for r, _, at, _ in tiles]
+        tops, prods = [], []
+        ahead = [score(tiles[0])]
+        for i, (r, bias, at, _) in enumerate(tiles):
+            if i + 1 < len(tiles):
+                ahead.append(score(tiles[i + 1]))
+            s = ahead[i] * scale2 + bias
+            top = jnp.max(s, axis=0, keepdims=True)
             if not fresh:
-                m_old = mx[h, r, 0:1, at]
-                m_new = jnp.maximum(m_old, m_new)
-            w = jnp.exp2(s - m_new).astype(jnp.bfloat16)
-            prod = jnp.dot(vals, w, preferred_element_type=jnp.float32)
-            if not fresh:
-                prod = acc[h, r, :, at] * jnp.exp2(m_old - m_new) + prod
-            acc[h, r, :, at] = prod
-            mx[h, r, 0:1, at] = m_new
-
-    def work(h, half, zs, seen, fresh=False):
-        update(h, half, 2 * half + 1, zs, False, fresh)
+                top = jnp.maximum(old[i], top)
+            w = jnp.exp2(s - top).astype(jnp.bfloat16)
+            prods.append(
+                jnp.dot(vals[:, :bias.shape[0]], w, preferred_element_type=jnp.float32)
+            )
+            tops.append(top)
+        for i, (r, _, at, _) in enumerate(tiles):
+            if fresh:
+                acc[h, r, :, at] = prods[i]
+            else:
+                acc[h, r, :, at] = acc[h, r, :, at] * jnp.exp2(old[i] - tops[i]) + prods[i]
+            mx[h, r, 0:1, at] = tops[i]
+
+    def work(h, half, zs, fresh=False):
         single = len(zs) == 1
-
-        if seen is None:
-            update(h, half, 2 * half, zs, not single, fresh)
-        else:
-            @pl.when(seen)
-            def _():
-                update(h, half, 2 * half, zs, not single, fresh)
-        if half == 0:
+        second, first = (2 * half + 1, False), (2 * half, not single)
+        crossing = (2, False)
+        if half == 1:
+            update(h, half, [second, first], zs, fresh)
+        elif fresh:
+            update(h, half, [second, first], zs, fresh)
+
             @pl.when(z == 0)
             def _():
-                update(h, 0, 2, zs, False, False)
+                update(h, half, [crossing], zs, False)
+        else:
+            @pl.when(z == 0)
+            def _():
+                update(h, half, [second, crossing], zs, fresh)
+
+            @pl.when(z != 0)
+            def _():
+                update(h, half, [second, first], zs, fresh)
 
     def finish(h):
         def one(r):
@@ -250,61 +269,66 @@
         lax.fori_loop(0, 2, lambda h, carry: (body(h), carry)[1], 0)
 
     def work_pair(h, half, s):
-        work(h, half, [(z + zn - s) % zn, (z + s) % zn], (z >= s) | (z + s >= zn))
+        work(h, half, [(z + zn - s) % zn, (z + s) % zn])
 
     start_ring(0)
     start_ring(1)
+    for h in range(2):
+        for d in range(1, XN):
+            q_copy(d, h).start()
+        q_own(h).start()
     find_starts()
     for h in range(2):
         for half in (1, 0):
             forward(h, half, 1)
     for h in range(2):
         wait_queries(h)
-
-    def first_step(h):
         for half in (1, 0):
-            work(h, half, [z], None, fresh=True)
-        for half in (1, 0):
-            work_pair(h, half, 1)
-
-    over_heads(first_step)
+            work(h, half, [z], fresh=True)
+
+    def pair_step(h, half, s):
+        @pl.when(s < half_ring - 1)
+        def _():
+            forward(h, half, s + 1)
+
+        work_pair(h, half, s)
 
     def step(s, carry):
-        def heads(h):
+        def heads(h, carry):
             for half in (1, 0):
-                forward(h, half, s)
-                work_pair(h, half, s)
-
-        over_heads(heads)
-        return carry
-
-    lax.fori_loop(2, half_ring, step, 0)
+                pair_step(h, half, s)
+            return carry
+
+        return lax.fori_loop(0, 2, heads, carry)
+
+    lax.fori_loop(1, half_ring, step, 0)
     far = (z + half_ring) % zn
 
-    for h in range(2):
-        for half in (1, 0):
-            (right if half == 0 else left)(h, half, half_ring - 1).wait_recv()
-            work(h, half, [far], z >= half_ring)
-        finish(h)
-
-    for h in range(2):
-        for d in range(1, XN):
-            o_copy(d, h).wait()
+    def drain(h, begin, end):
+        for copy, steps in ((right, right_steps), (left, left_steps)):
+            for half in range(2):
+                def wait_one(s, carry):
+                    copy(h, half, s).wait_send()
+                    return carry
+
+                lax.fori_loop(begin, end or steps[half], wait_one, 0)
+
+    for h in range(2):
+        drain(h, 0, half_ring - 1)
+        for d in range(1, XN):
             q_copy(d, h).wait_send()
             for which in range(2):
                 kv_copy(d, h, which).wait_send()
+    for h in range(2):
+        for half in (1, 0):
+            (right if half == 0 else left)(h, half, half_ring - 1).wait_recv()
+            work(h, half, [far])
+        finish(h)
+    for h in range(2):
+        drain(h, half_ring - 1, None)
+        for d in range(1, XN):
+            o_copy(d, h).wait()
         o_own(h).wait()
-        for half in range(2):
-            def drain_right(s, carry):
-                right(h, half, s).wait_send()
-                return carry
-
-            def drain_left(s, carry):
-                left(h, half, s).wait_send()
-                return carry
-
-            lax.fori_loop(0, right_steps[half], drain_right, 0)
-            lax.fori_loop(0, left_steps[half], drain_left, 0)
 
 
 def per_device(queries, keys, values, doc_lengths):
@@ -315,8 +339,8 @@
     return pl.pallas_call(
         functools.partial(kernel, zn, tok),
         out_shape=jax.ShapeDtypeStruct(queries.shape, jnp.bfloat16),
-        in_specs=[pl.BlockSpec(memory_space=pltpu.VMEM)] * 4,
-        out_specs=pl.BlockSpec(memory_space=pltpu.VMEM),
+        in_specs=[pl.BlockSpec(memory_space=pl.ANY)] * 3 + [pl.BlockSpec(memory_space=pltpu.VMEM)],
+        out_specs=pl.BlockSpec(memory_space=pl.ANY),
         scratch_shapes=[
             vmem((2, XN, tok, kvw), jnp.bfloat16),
             vmem((2, 2, zn, 2, 2, tok, HD), jnp.bfloat16),

time: 88.9 us -> 82.2 us (0.925)
  Pallas kernels: 85.9 us -> 79.8 us
    pallas_call x1, Pallas kernels: 85.9 us -> 79.8 us  [per_device(): pl.pallas_call(functools.partial(kernel, zn, tok), out_shape=jax.ShapeDty...]
where the time goes in v3:
time: 82.2 us; the launch traced here: 82 us
  Pallas kernels  79.8 us (97%)
  local copies, waits for them, and re-layouts  2.26 us (3%)
    pallas_call x1, Pallas kernels, per_device(): pl.pallas_call(functools.partial(kernel, zn, tok), out_shape=jax.ShapeDty...  79.8 us
    unnamed x1, local copies, waits for them, and re-layouts  2.26 us

profile of v3, /device:TPU:24, one launch (start us, length us, event | category | flops | bytes accessed | tf_op | source)
XLA Modules:
  0.0 82.0 jit_solution(1894336899005063233)
XLA Ops:
  0.0 79.8 %ring_attention.1 = bf16[1,64,8192]{2,1,0:T(8,128)(2,1)} custom-call(bf16[1,64,8192]{2,1,0:T(8,128)(2,1)} %q_ref.1, bf16[1,64,1024]{2,1,0:T(8,128)(2,1)} %k_ref.1, bf16[1,64,1024]{2,1,0:T(8,128)(2,1)} %v_ref.1, s32[8,129]{1,0:T(8,128)} %len_ref.1), custom_call_target="tpu_custom_call" | custom-call | tf_op jit(solution)/shard_map/ring_attention/pallas_call | solution.py:339
  79.8 2.3 %copy.6 = bf16[1,64,8192]{2,1,0:T(8,128)(2,1)} copy(bf16[1,64,8192]{2,1,0:T(8,128)(2,1)} %ring_attention.1) | data formatting | bytes 2097152

commit v4 on v3

--- a/solution.py
+++ b/solution.py
@@ -237,20 +237,17 @@
             def _():
                 update(h, half, [second, first], zs, fresh)
 
-    def finish(h):
-        def one(r):
-            o = acc[h, r, :HD, :] / acc[h, r, HD:HD + 1, :]
-            for i in range(GROUP):
-                obuf[h, r, :, i * HD:(i + 1) * HD] = (
-                    o[:, i * tok:(i + 1) * tok].T.astype(jnp.bfloat16)
-                )
-
-        for d in (2, 1, 3, 0):
-            one(peer(d))
-            if d:
-                o_copy(d, h).start()
-            else:
-                o_own(h).start()
+    def finish(h, r):
+        o = acc[h, r, :HD, :] / acc[h, r, HD:HD + 1, :]
+        for i in range(GROUP):
+            obuf[h, r, :, i * HD:(i + 1) * HD] = o[:, i * tok:(i + 1) * tok].T.astype(jnp.bfloat16)
+        for d in range(XN):
+            @pl.when(peer(d) == r)
+            def _():
+                if d:
+                    o_copy(d, h).start()
+                else:
+                    o_own(h).start()
 
     right_steps = (half_ring, half_ring - 1)
     left_steps = (half_ring - 1, half_ring)
@@ -278,16 +275,18 @@
             q_copy(d, h).start()
         q_own(h).start()
     find_starts()
-    for h in range(2):
-        for half in (1, 0):
-            forward(h, half, 1)
+    ahead = min(2, half_ring - 1)
+    for s in range(1, ahead + 1):
+        for h in range(2):
+            for half in range(2):
+                forward(h, half, s)
     for h in range(2):
         wait_queries(h)
         for half in (1, 0):
             work(h, half, [z], fresh=True)
 
     def pair_step(h, half, s):
-        @pl.when(s < half_ring - 1)
+        @pl.when((s >= ahead) & (s < half_ring - 1))
         def _():
             forward(h, half, s + 1)
 
@@ -295,7 +294,7 @@
 
     def step(s, carry):
         def heads(h, carry):
-            for half in (1, 0):
+            for half in range(2):
                 pair_step(h, half, s)
             return carry
 
@@ -320,10 +319,11 @@
             for which in range(2):
                 kv_copy(d, h, which).wait_send()
     for h in range(2):
-        for half in (1, 0):
+        for half in range(2):
             (right if half == 0 else left)(h, half, half_ring - 1).wait_recv()
             work(h, half, [far])
-        finish(h)
+            for r in (2 * half + 1, 2 * half):
+                finish(h, r)
     for h in range(2):
         drain(h, half_ring - 1, None)
         for d in range(1, XN):

time: 82.2 us -> 77.7 us (0.945)
  Pallas kernels: 79.8 us -> 75.2 us
    pallas_call x1, Pallas kernels: 79.8 us -> 75.2 us  [per_device(): pl.pallas_call(functools.partial(kernel, zn, tok), out_shape=jax.ShapeDty...]
where the time goes in v4:
time: 77.7 us; the launch traced here: 77.5 us
  Pallas kernels  75.2 us (97%)
  local copies, waits for them, and re-layouts  2.26 us (3%)
    pallas_call x1, Pallas kernels, per_device(): pl.pallas_call(functools.partial(kernel, zn, tok), out_shape=jax.ShapeDty...  75.2 us
    unnamed x1, local copies, waits for them, and re-layouts  2.26 us

profile of v4, /device:TPU:24, one launch (start us, length us, event | category | flops | bytes accessed | tf_op | source)
XLA Modules:
  0.0 77.5 jit_solution(12890379560405891934)
XLA Ops:
  0.0 75.2 %ring_attention.1 = bf16[1,64,8192]{2,1,0:T(8,128)(2,1)} custom-call(bf16[1,64,8192]{2,1,0:T(8,128)(2,1)} %q_ref.1, bf16[1,64,1024]{2,1,0:T(8,128)(2,1)} %k_ref.1, bf16[1,64,1024]{2,1,0:T(8,128)(2,1)} %v_ref.1, s32[8,129]{1,0:T(8,128)} %len_ref.1), custom_call_target="tpu_custom_call" | custom-call | tf_op jit(solution)/shard_map/ring_attention/pallas_call | solution.py:339
  75.2 2.3 %copy.6 = bf16[1,64,8192]{2,1,0:T(8,128)(2,1)} copy(bf16[1,64,8192]{2,1,0:T(8,128)(2,1)} %ring_attention.1) | data formatting | bytes 2097152

commit v5 on v4

--- a/solution.py
+++ b/solution.py
@@ -270,9 +270,9 @@
 
     start_ring(0)
     start_ring(1)
-    for h in range(2):
-        for d in range(1, XN):
-            q_copy(d, h).start()
+    for d in range(1, XN):
+        q_copy(d, 0).start()
+    for h in range(2):
         q_own(h).start()
     find_starts()
     ahead = min(2, half_ring - 1)
@@ -280,6 +280,9 @@
         for h in range(2):
             for half in range(2):
                 forward(h, half, s)
+        if s == 1:
+            for d in range(1, XN):
+                q_copy(d, 1).start()
     for h in range(2):
         wait_queries(h)
         for half in (1, 0):

time: 77.7 us -> 77 us (level)
  no operation moved by 1% of the time
where the time goes in v5:
time: 77 us; the launch traced here: 76.8 us
  Pallas kernels  74.6 us (97%)
  local copies, waits for them, and re-layouts  2.26 us (3%)
    pallas_call x1, Pallas kernels, per_device(): pl.pallas_call(functools.partial(kernel, zn, tok), out_shape=jax.ShapeDty...  74.6 us
    unnamed x1, local copies, waits for them, and re-layouts  2.26 us

profile of v5, /device:TPU:24, one launch (start us, length us, event | category | flops | bytes accessed | tf_op | source)
XLA Modules:
  0.0 76.8 jit_solution(15230576089765913565)
XLA Ops:
  0.0 74.6 %ring_attention.1 = bf16[1,64,8192]{2,1,0:T(8,128)(2,1)} custom-call(bf16[1,64,8192]{2,1,0:T(8,128)(2,1)} %q_ref.1, bf16[1,64,1024]{2,1,0:T(8,128)(2,1)} %k_ref.1, bf16[1,64,1024]{2,1,0:T(8,128)(2,1)} %v_ref.1, s32[8,129]{1,0:T(8,128)} %len_ref.1), custom_call_target="tpu_custom_call" | custom-call | tf_op jit(solution)/shard_map/ring_attention/pallas_call | solution.py:342
  74.6 2.3 %copy.6 = bf16[1,64,8192]{2,1,0:T(8,128)(2,1)} copy(bf16[1,64,8192]{2,1,0:T(8,128)(2,1)} %ring_attention.1) | data formatting | bytes 2097152
